TPU v7x, 32 devices: a whole 2x2x4 slice. The times are simulated.
32 devices in a mesh: dp: 8 (over y, x, core), seq: 4 (over z).
Axes of the slice: x: 2, y: 2, z: 4, core: 2. Of those that a mesh axis runs over, the one named last changes fastest.
Arguments:
- inputs: bfloat16 [24, 1024, 768], P('dp', 'seq'), may hold values from -6 to 6
- segment_ids: int32 [24, 1024], P('dp', 'seq'), may hold values from 0 to 3, never falling along the last dimension, each value on 1 to 512 neighbouring positions
- norm1_gain: bfloat16 [768], P('dp'), may hold values from 0.5 to 1.5
- norm1_shift: bfloat16 [768], P('dp'), may hold values from -1.5 to 1.5
- query_weight: bfloat16 [768, 768], P('dp'), may hold values from -0.4375 to 0.4375
- query_bias: bfloat16 [768], P('dp'), may hold values from -2.5 to 2.5
- key_weight: bfloat16 [768, 768], P('dp'), may hold values from -0.21875 to 0.21875
- value_weight: bfloat16 [768, 768], P('dp'), may hold values from -0.21875 to 0.21875
- value_bias: bfloat16 [768], P('dp'), may hold values from -1.5 to 1.5
- out_weight: bfloat16 [768, 768], P('dp'), may hold values from -0.625 to 0.625
- out_bias: bfloat16 [768], P('dp'), may hold values from -1.5 to 1.5
- norm2_gain: bfloat16 [768], P('dp'), may hold values from 0.5 to 1.5
- norm2_shift: bfloat16 [768], P('dp'), may hold values from -1.5 to 1.5
- fc1_weight: bfloat16 [768, 3072], P('dp'), may hold values from -0.21875 to 0.21875
- fc1_bias: bfloat16 [3072], P('dp'), may hold values from -1.5 to 1.5
- fc2_weight: bfloat16 [3072, 768], P('dp'), may hold values from -0.15625 to 0.15625
- fc2_bias: bfloat16 [768], P('dp'), may hold values from -1.5 to 1.5
- grad_output: bfloat16 [24, 1024, 768], P('dp', 'seq'), may hold values from -6 to 6
Outputs:
- output: bfloat16 [24, 1024, 768], P('dp', 'seq')
- grad_inputs: bfloat16 [24, 1024, 768], P('dp', 'seq')
- grad_norm1_gain: float32 [768], P('dp')
- grad_norm1_shift: float32 [768], P('dp')
- grad_query_weight: float32 [768, 768], P('dp')
- grad_query_bias: float32 [768], P('dp')
- grad_key_weight: float32 [768, 768], P('dp')
- grad_value_weight: float32 [768, 768], P('dp')
- grad_value_bias: float32 [768], P('dp')
- grad_out_weight: float32 [768, 768], P('dp')
- grad_out_bias: float32 [768], P('dp')
- grad_norm2_gain: float32 [768], P('dp')
- grad_norm2_shift: float32 [768], P('dp')
- grad_fc1_weight: float32 [768, 3072], P('dp')
- grad_fc1_bias: float32 [3072], P('dp')
- grad_fc2_weight: float32 [3072, 768], P('dp')
- grad_fc2_bias: float32 [768], P('dp')
Inputs may be any that keep to these rules, and one draw needn't show every extreme that they name: `segment_ids`: within each sequence, segment numbers never fall along the positions; each segment is a run of 1 to 512 positions.
All inputs are finite; a program needn't handle non-finite values.
Results may differ from a plain program's by a relative error of at most 0.017.
Values may be sent and summed in bfloat16 or wider, within the bound.
No kernel may reach another device: no remote copies, remote signals or barrier semaphores. Data moves between devices by JAX's collectives and lax.ppermute only.
A program may use at most 192 MiB of HBM per device.

v0:
```python
import jax
import jax.numpy as jnp
from jax import lax
from jax.sharding import PartitionSpec as P

HD = 64
EPSILON = 1e-05


def layer_norm(values, gain, shift):
    center = values - jnp.mean(values, axis=-1, keepdims=True)
    inverse = lax.rsqrt(jnp.mean(center * center, axis=-1, keepdims=True) + EPSILON)
    normed = center * inverse
    return (normed * gain + shift, normed, inverse)


def norm_back(grad, normed, inverse, gain):
    scaled = grad * gain
    return inverse * (
        scaled
        - jnp.mean(scaled, axis=-1, keepdims=True)
        - normed * jnp.mean(scaled * normed, axis=-1, keepdims=True)
    )


def gelu_slope(pre_act):
    return (
        0.5 * (1.0 + lax.erf(pre_act * 0.7071067811865476))
        + pre_act * jnp.exp(-0.5 * pre_act * pre_act) * 0.3989422804014327
    )


def cross_rows(left, right):
    return lax.dot_general(
        left, right, (((0,), (0,)), ((), ())), preferred_element_type=jnp.float32
    )


def times_transpose(left, right):
    return lax.dot_general(
        left, right, (((1,), (1,)), ((), ())), preferred_element_type=jnp.float32
    )


def to_pairs(array, heads_here):
    seqs_here, positions, _ = array.shape
    shaped = array.reshape(seqs_here, positions, heads_here, HD).transpose(0, 2, 1, 3)
    return shaped.reshape(seqs_here * heads_here, positions, HD)


def from_pairs(array, seqs_here, heads_here):
    positions = array.shape[1]
    shaped = array.reshape(seqs_here, heads_here, positions, HD).transpose(0, 2, 1, 3)
    return shaped.reshape(seqs_here, positions, heads_here * HD)


def masked_scores(query_pair, key_pair, segment_row):
    scores = jnp.einsum(
        "qd,kd->qk", query_pair, key_pair, preferred_element_type=jnp.float32
    ) * HD ** (-0.5)
    same_segment = segment_row[:, None] == segment_row[None, :]
    return jnp.where(same_segment, scores, -1e30)


def attend_forward(packed):
    query_pair, key_pair, value_pair, segment_row = packed
    scores = masked_scores(query_pair, key_pair, segment_row)
    highest = jnp.max(scores, axis=-1, keepdims=True)
    expon = jnp.exp(scores - highest)
    totals = jnp.sum(expon, axis=-1, keepdims=True)
    probs = (expon / totals).astype(jnp.bfloat16)
    result = jnp.dot(probs, value_pair, preferred_element_type=jnp.float32).astype(jnp.bfloat16)
    return (result, (highest + jnp.log(totals))[:, 0])


def attend_backward(packed):
    query_pair, key_pair, value_pair, segment_row, logsum, grad_pair = packed
    scores = masked_scores(query_pair, key_pair, segment_row)
    probs = jnp.exp(scores - logsum[:, None])
    grad_probs = jnp.einsum("qd,kd->qk", grad_pair, value_pair, preferred_element_type=jnp.float32)
    delta = jnp.sum(probs * grad_probs, axis=-1, keepdims=True)
    grad_scores = (probs * (grad_probs - delta)).astype(jnp.bfloat16)
    factor = HD ** (-0.5)
    grad_query = (
        jnp.einsum("qk,kd->qd", grad_scores, key_pair, preferred_element_type=jnp.float32) * factor
    ).astype(jnp.bfloat16)
    grad_key = (
        jnp.einsum("qk,qd->kd", grad_scores, query_pair, preferred_element_type=jnp.float32)
        * factor
    ).astype(jnp.bfloat16)
    grad_value = jnp.einsum(
        "qk,qd->kd", probs.astype(jnp.bfloat16), grad_pair, preferred_element_type=jnp.float32
    ).astype(jnp.bfloat16)
    return (grad_query, grad_key, grad_value)


def column_sum(array):
    return jnp.sum(array.astype(jnp.float32), axis=0)


def per_device(
    inputs,
    segment_ids,
    norm1_gain,
    norm1_shift,
    query_weight,
    query_bias,
    key_weight,
    value_weight,
    value_bias,
    out_weight,
    out_bias,
    norm2_gain,
    norm2_shift,
    fc1_weight,
    fc1_bias,
    fc2_weight,
    fc2_bias,
    grad_output,
):
    seqs_here, positions, model_width = inputs.shape
    token_rows = seqs_here * positions
    (
        first_gain,
        first_shift,
        w_query,
        b_query,
        w_key,
        w_value,
        b_value,
        w_out,
        b_out,
        second_gain,
        second_shift,
        w_up,
        b_up,
        w_down,
        b_down,
    ) = (
        lax.all_gather(norm1_gain, "dp", axis=0, tiled=True),
        lax.all_gather(norm1_shift, "dp", axis=0, tiled=True),
        lax.all_gather(query_weight, "dp", axis=0, tiled=True),
        lax.all_gather(query_bias, "dp", axis=0, tiled=True),
        lax.all_gather(key_weight, "dp", axis=0, tiled=True),
        lax.all_gather(value_weight, "dp", axis=0, tiled=True),
        lax.all_gather(value_bias, "dp", axis=0, tiled=True),
        lax.all_gather(out_weight, "dp", axis=0, tiled=True),
        lax.all_gather(out_bias, "dp", axis=0, tiled=True),
        lax.all_gather(norm2_gain, "dp", axis=0, tiled=True),
        lax.all_gather(norm2_shift, "dp", axis=0, tiled=True),
        lax.all_gather(fc1_weight, "dp", axis=0, tiled=True),
        lax.all_gather(fc1_bias, "dp", axis=0, tiled=True),
        lax.all_gather(fc2_weight, "dp", axis=0, tiled=True),
        lax.all_gather(fc2_bias, "dp", axis=0, tiled=True),
    )
    full_segments = lax.all_gather(segment_ids, "seq", axis=1, tiled=True)
    flat_in = inputs.reshape(token_rows, model_width).astype(jnp.float32)
    normed_one, unit_one, inverse_one = layer_norm(
        flat_in, first_gain.astype(jnp.float32), first_shift.astype(jnp.float32)
    )
    act_one = normed_one.astype(jnp.bfloat16)
    query_tok = (
        jnp.dot(act_one, w_query, preferred_element_type=jnp.float32) + b_query.astype(jnp.float32)
    ).astype(jnp.bfloat16)
    key_tok = jnp.dot(act_one, w_key, preferred_element_type=jnp.float32).astype(jnp.bfloat16)
    value_tok = (
        jnp.dot(act_one, w_value, preferred_element_type=jnp.float32) + b_value.astype(jnp.float32)
    ).astype(jnp.bfloat16)
    query_heads, key_heads, value_heads = (
        lax.all_to_all(
            query_tok.reshape(seqs_here, positions, model_width),
            "seq",
            split_axis=2,
            concat_axis=1,
            tiled=True,
        ),
        lax.all_to_all(
            key_tok.reshape(seqs_here, positions, model_width),
            "seq",
            split_axis=2,
            concat_axis=1,
            tiled=True,
        ),
        lax.all_to_all(
            value_tok.reshape(seqs_here, positions, model_width),
            "seq",
            split_axis=2,
            concat_axis=1,
            tiled=True,
        ),
    )
    heads_here = query_heads.shape[2] // HD
    query_pairs = to_pairs(query_heads, heads_here)
    key_pairs = to_pairs(key_heads, heads_here)
    value_pairs = to_pairs(value_heads, heads_here)
    segment_pairs = jnp.repeat(full_segments, heads_here, axis=0)
    attn_pairs, logsum = lax.map(
        attend_forward, (query_pairs, key_pairs, value_pairs, segment_pairs)
    )
    attn_heads = from_pairs(attn_pairs, seqs_here, heads_here)
    attn_tok = lax.all_to_all(attn_heads, "seq", split_axis=1, concat_axis=2, tiled=True).reshape(
        token_rows, model_width
    )
    middle = (
        flat_in
        + jnp.dot(attn_tok, w_out, preferred_element_type=jnp.float32)
        + b_out.astype(jnp.float32)
    )
    normed_two, unit_two, inverse_two = layer_norm(
        middle, second_gain.astype(jnp.float32), second_shift.astype(jnp.float32)
    )
    act_two = normed_two.astype(jnp.bfloat16)
    pre_act = jnp.dot(act_two, w_up, preferred_element_type=jnp.float32) + b_up.astype(jnp.float32)
    hidden = jax.nn.gelu(pre_act, approximate=False).astype(jnp.bfloat16)
    result = (
        middle
        + jnp.dot(hidden, w_down, preferred_element_type=jnp.float32)
        + b_down.astype(jnp.float32)
    )
    output = result.astype(jnp.bfloat16).reshape(seqs_here, positions, model_width)
    first_gain_b, w_query_b, w_key_b, w_value_b, w_out_b, second_gain_b, w_up_b, w_down_b = (
        lax.all_gather(norm1_gain, "dp", axis=0, tiled=True),
        lax.all_gather(query_weight, "dp", axis=0, tiled=True),
        lax.all_gather(key_weight, "dp", axis=0, tiled=True),
        lax.all_gather(value_weight, "dp", axis=0, tiled=True),
        lax.all_gather(out_weight, "dp", axis=0, tiled=True),
        lax.all_gather(norm2_gain, "dp", axis=0, tiled=True),
        lax.all_gather(fc1_weight, "dp", axis=0, tiled=True),
        lax.all_gather(fc2_weight, "dp", axis=0, tiled=True),
    )
    grad_down = grad_output.reshape(token_rows, model_width)
    d_b_down = column_sum(grad_down)
    d_w_down = cross_rows(hidden, grad_down)
    grad_hidden = times_transpose(grad_down, w_down_b)
    grad_pre = (grad_hidden * gelu_slope(pre_act)).astype(jnp.bfloat16)
    d_b_up = column_sum(grad_pre)
    d_w_up = cross_rows(act_two, grad_pre)
    grad_two = times_transpose(grad_pre, w_up_b)
    d_second_gain = jnp.sum(grad_two * unit_two, axis=0)
    d_second_shift = jnp.sum(grad_two, axis=0)
    grad_middle = grad_down.astype(jnp.float32) + norm_back(
        grad_two, unit_two, inverse_two, second_gain_b.astype(jnp.float32)
    )
    grad_branch = grad_middle.astype(jnp.bfloat16)
    d_b_out = column_sum(grad_branch)
    d_w_out = cross_rows(attn_tok, grad_branch)
    grad_attn = (
        times_transpose(grad_branch, w_out_b)
        .astype(jnp.bfloat16)
        .reshape(seqs_here, positions, model_width)
    )
    grad_attn_heads = lax.all_to_all(grad_attn, "seq", split_axis=2, concat_axis=1, tiled=True)
    grad_query_pairs, grad_key_pairs, grad_value_pairs = lax.map(
        attend_backward,
        (
            query_pairs,
            key_pairs,
            value_pairs,
            segment_pairs,
            logsum,
            to_pairs(grad_attn_heads, heads_here),
        ),
    )
    grad_query_tok, grad_key_tok, grad_value_tok = (
        lax.all_to_all(
            from_pairs(grad_query_pairs, seqs_here, heads_here),
            "seq",
            split_axis=1,
            concat_axis=2,
            tiled=True,
        ),
        lax.all_to_all(
            from_pairs(grad_key_pairs, seqs_here, heads_here),
            "seq",
            split_axis=1,
            concat_axis=2,
            tiled=True,
        ),
        lax.all_to_all(
            from_pairs(grad_value_pairs, seqs_here, heads_here),
            "seq",
            split_axis=1,
            concat_axis=2,
            tiled=True,
        ),
    )
    grad_query_tok = grad_query_tok.reshape(token_rows, model_width)
    grad_key_tok = grad_key_tok.reshape(token_rows, model_width)
    grad_value_tok = grad_value_tok.reshape(token_rows, model_width)
    d_b_query = column_sum(grad_query_tok)
    d_b_value = column_sum(grad_value_tok)
    d_w_query = cross_rows(act_one, grad_query_tok)
    d_w_key = cross_rows(act_one, grad_key_tok)
    d_w_value = cross_rows(act_one, grad_value_tok)
    grad_one = (
        times_transpose(grad_query_tok, w_query_b)
        + times_transpose(grad_key_tok, w_key_b)
        + times_transpose(grad_value_tok, w_value_b)
    )
    d_first_gain = jnp.sum(grad_one * unit_one, axis=0)
    d_first_shift = jnp.sum(grad_one, axis=0)
    grad_inputs = grad_middle + norm_back(
        grad_one, unit_one, inverse_one, first_gain_b.astype(jnp.float32)
    )
    grad_inputs = grad_inputs.astype(jnp.bfloat16).reshape(seqs_here, positions, model_width)
    (
        part_first_gain,
        part_first_shift,
        part_w_query,
        part_b_query,
        part_w_key,
        part_w_value,
        part_b_value,
        part_w_out,
        part_b_out,
        part_second_gain,
        part_second_shift,
        part_w_up,
        part_b_up,
        part_w_down,
        part_b_down,
    ) = (
        lax.psum_scatter(d_first_gain, "dp", scatter_dimension=0, tiled=True),
        lax.psum_scatter(d_first_shift, "dp", scatter_dimension=0, tiled=True),
        lax.psum_scatter(d_w_query, "dp", scatter_dimension=0, tiled=True),
        lax.psum_scatter(d_b_query, "dp", scatter_dimension=0, tiled=True),
        lax.psum_scatter(d_w_key, "dp", scatter_dimension=0, tiled=True),
        lax.psum_scatter(d_w_value, "dp", scatter_dimension=0, tiled=True),
        lax.psum_scatter(d_b_value, "dp", scatter_dimension=0, tiled=True),
        lax.psum_scatter(d_w_out, "dp", scatter_dimension=0, tiled=True),
        lax.psum_scatter(d_b_out, "dp", scatter_dimension=0, tiled=True),
        lax.psum_scatter(d_second_gain, "dp", scatter_dimension=0, tiled=True),
        lax.psum_scatter(d_second_shift, "dp", scatter_dimension=0, tiled=True),
        lax.psum_scatter(d_w_up, "dp", scatter_dimension=0, tiled=True),
        lax.psum_scatter(d_b_up, "dp", scatter_dimension=0, tiled=True),
        lax.psum_scatter(d_w_down, "dp", scatter_dimension=0, tiled=True),
        lax.psum_scatter(d_b_down, "dp", scatter_dimension=0, tiled=True),
    )
    (
        shard_first_gain,
        shard_first_shift,
        shard_w_query,
        shard_b_query,
        shard_w_key,
        shard_w_value,
        shard_b_value,
        shard_w_out,
        shard_b_out,
        shard_second_gain,
        shard_second_shift,
        shard_w_up,
        shard_b_up,
        shard_w_down,
        shard_b_down,
    ) = (
        lax.psum(part_first_gain.astype(jnp.bfloat16), "seq").astype(jnp.float32),
        lax.psum(part_first_shift.astype(jnp.bfloat16), "seq").astype(jnp.float32),
        lax.psum(part_w_query.astype(jnp.bfloat16), "seq").astype(jnp.float32),
        lax.psum(part_b_query.astype(jnp.bfloat16), "seq").astype(jnp.float32),
        lax.psum(part_w_key.astype(jnp.bfloat16), "seq").astype(jnp.float32),
        lax.psum(part_w_value.astype(jnp.bfloat16), "seq").astype(jnp.float32),
        lax.psum(part_b_value.astype(jnp.bfloat16), "seq").astype(jnp.float32),
        lax.psum(part_w_out.astype(jnp.bfloat16), "seq").astype(jnp.float32),
        lax.psum(part_b_out.astype(jnp.bfloat16), "seq").astype(jnp.float32),
        lax.psum(part_second_gain.astype(jnp.bfloat16), "seq").astype(jnp.float32),
        lax.psum(part_second_shift.astype(jnp.bfloat16), "seq").astype(jnp.float32),
        lax.psum(part_w_up.astype(jnp.bfloat16), "seq").astype(jnp.float32),
        lax.psum(part_b_up.astype(jnp.bfloat16), "seq").astype(jnp.float32),
        lax.psum(part_w_down.astype(jnp.bfloat16), "seq").astype(jnp.float32),
        lax.psum(part_b_down.astype(jnp.bfloat16), "seq").astype(jnp.float32),
    )
    return (
        output,
        grad_inputs,
        shard_first_gain,
        shard_first_shift,
        shard_w_query,
        shard_b_query,
        shard_w_key,
        shard_w_value,
        shard_b_value,
        shard_w_out,
        shard_b_out,
        shard_second_gain,
        shard_second_shift,
        shard_w_up,
        shard_b_up,
        shard_w_down,
        shard_b_down,
    )


def solution(mesh):
    placed = (
        P("dp", "seq", None),
        P("dp", "seq"),
        P("dp"),
        P("dp"),
        P("dp", None),
        P("dp"),
        P("dp", None),
        P("dp", None),
        P("dp"),
        P("dp", None),
        P("dp"),
        P("dp"),
        P("dp"),
        P("dp", None),
        P("dp"),
        P("dp", None),
        P("dp"),
        P("dp", "seq", None),
    )
    return jax.shard_map(
        per_device,
        mesh=mesh,
        in_specs=placed,
        out_specs=(
            P("dp", "seq", None),
            P("dp", "seq", None),
            P("dp"),
            P("dp"),
            P("dp", None),
            P("dp"),
            P("dp", None),
            P("dp", None),
            P("dp"),
            P("dp", None),
            P("dp"),
            P("dp"),
            P("dp"),
            P("dp", None),
            P("dp"),
            P("dp", None),
            P("dp"),
        ),
        check_vma=False,
    )
```

profile of v0, /device:TPU:0, one launch (start us, length us, event | category | flops | bytes accessed | tf_op | source)
XLA Modules:
  0.0 1093.1 jit_solution(9284306337476619404)
XLA Ops:
  15.2 26.3 %all-reduce.18 = (bf16[768]{0:T(1024)(128)(2,1)S(1)}, bf16[768]{0:T(1024)(128)(2,1)S(1)}, bf16[768]{0:T(1024)(128)(2,1)S(1)}, bf16[768]{0:T(1024)(128)(2,1)S(1)}...) all-reduce(bf16[768]{0:T(1024)(128)(2,1)S(1)} %dynamic-update-slice, ...), channel_id=1, replica_groups=mesh['dp'=8,'seq'=4] {'dp'}, use_global_device_ids=true, to_apply=%add.1 | all-reduce | flops 6144 | bytes 24576
  47.7 5.0 all-to-all-start
  53.4 9.6 all-gather.12.cloned.1.call-done
  70.2 16.2 %all-to-all-done = bf16[3,256,768]{1,0,2:T(4,128)(2,1)S(1)} async-done(((bf16[3,256,768]{1,0,2:T(4,128)(2,1)}), bf16[3,256,768]{1,0,2:T(4,128)(2,1)S(1)}, u32[]{:S(2)}, u32[]{:S(2)}) %all-to-all-start) | async-done | bytes 1179680 | tf_op jit(solution)/shard_map/all_to_all | solution.py:170
  98.7 28.6 %all-to-all-done.2 = bf16[3,256,768]{1,0,2:T(4,128)(2,1)} async-done(((bf16[3,256,768]{1,0,2:T(4,128)(2,1)}), bf16[3,256,768]{1,0,2:T(4,128)(2,1)}, u32[]{:S(2)}, u32[]{:S(2)}) %all-to-all-start.2) | async-done | bytes 1179680 | tf_op jit(solution)/shard_map/all_to_all | solution.py:184
  132.3 41.2 %all_gather.56 = s32[3,1024]{1,0:T(4,128)S(1)} all-gather(s32[3,256]{1,0:T(4,128)S(1)} %copy-done.26), channel_id=1, replica_groups=mesh['dp'=8,'seq'=4] {'seq'}, dimensions={1}, use_global_device_ids=true | all-gather | bytes 15360 | tf_op jit(solution)/shard_map/all_gather | solution.py:156
  202.1 99.2 %while.26 = (s32[]{:T(128)}, bf16[9,1024,64]{1,2,0:T(8,128)(2,1)}, f32[9,1024]{1,0:T(8,128)}, s32[9,1024]{1,0:T(8,128)}, bf16[9,1024,64]{2,1,0:T(8,128)(2,1)S(1)...) while((s32[]{:T(128)}, bf16[9,1024,64]{1,2,0:T(8,128)(2,1)}, ...), condition=%wide.region_5.6_spmd, body=%wide.region_2.5_spmd.sunk | while | flops 284228608 | bytes 30349440 | solution.py:197
  311.4 10.1 all-gather
  322.1 33.6 %all-to-all-done.3 = bf16[3,1024,192]{2,0,1:T(4,128)(2,1)} async-done(((bf16[3,1024,192]{2,0,1:T(4,128)(2,1)}), bf16[3,1024,192]{2,0,1:T(4,128)(2,1)}, u32[]{:S(2)}, u32[]{:S(2)}) %all-to-all-start.3) | async-done | bytes 1179680 | tf_op jit(solution)/shard_map/all_to_all | solution.py:201
  364.3 27.2 %fusion.56 = (bf16[768,3072]{1,0:T(8,128)(2,1)}, f32[768,3072]{1,0:T(8,128)}) fusion(f32[3072]{0:T(1024)} %bitcast.275, bf16[768,3072]{1,0:T(8,128)(2,1)} %all-gather.16.cloned.1.call-done, f32[768,768]{1,0:T(8,128)S(1)} %get-tuple-element.265, f32[768]{0:T(1024)S(1)} %convert_element_type.227, f32[768]{0:T(1024)S(1)} %convert_element_type.226, ...), kind=kOutput, calls=%fused_computation.64 | convolution fusion | flops 3782541312 | bytes 21258240 | tf_op jit(solution)/shard_map/dot_general | solution.py:213
  391.5 11.6 %convert_reduce_fusion = (f32[3072]{0:T(1024)}, bf16[768,3072]{1,0:T(8,128)(2,1)S(1)}) fusion(f32[768,3072]{1,0:T(8,128)} %get-tuple-element.267, f32[3072]{0:T(1024)} %bitcast.276, bf16[768,768]{1,0:T(8,128)(2,1)} %bitcast.249, bf16[3072,768]{1,0:T(8,128)(2,1)} %all-gather.18.cloned.1.call-done), kind=kOutput, calls=%fused_computation.71 | convolution fusion | flops 3654546432 | bytes 20078592 | tf_op jit(solution)/shard_map/dot_general | solution.py:40
  424.4 31.9 %all-to-all-done.4 = bf16[3,256,768]{1,0,2:T(4,128)(2,1)} async-done(((bf16[3,256,768]{1,0,2:T(4,128)(2,1)}), bf16[3,256,768]{1,0,2:T(4,128)(2,1)}, u32[]{:S(2)}, u32[]{:S(2)}) %all-to-all-start.4) | async-done | bytes 1179680 | tf_op jit(solution)/shard_map/all_to_all | solution.py:252
  467.1 124.2 %while.27 = (s32[]{:T(128)}, bf16[9,1024,64]{1,2,0:T(8,128)(2,1)}, bf16[9,1024,64]{1,2,0:T(8,128)(2,1)}, bf16[9,1024,64]{1,2,0:T(8,128)(2,1)}, s32[9,1024]{1,0:T...) while((s32[]{:T(128)}, bf16[9,1024,64]{1,2,0:T(8,128)(2,1)}, ...), condition=%wide.region_12.13_spmd, body=%wide.region_10.12_spmd.sunk | while | flops 681901056 | bytes 33465460 | solution.py:253
  602.0 45.4 %all-to-all-done.5 = bf16[3,1024,192]{2,0,1:T(4,128)(2,1)} async-done(((bf16[3,1024,192]{2,0,1:T(4,128)(2,1)}), bf16[3,1024,192]{2,0,1:T(4,128)(2,1)}, u32[]{:S(2)}, u32[]{:S(2)}) %all-to-all-start.5) | async-done | bytes 1179680 | tf_op jit(solution)/shard_map/all_to_all | solution.py:265
  664.0 51.4 %all_to_all.120 = bf16[3,1024,192]{2,0,1:T(4,128)(2,1)S(1)} all-to-all(bf16[3,1024,192]{2,0,1:T(4,128)(2,1)} %copy.125), channel_id=1, replica_groups=mesh['dp'=8,'seq'=4] {'seq'}, dimensions={1} | all-to-all | bytes 2359296 | tf_op jit(solution)/shard_map/all_to_all | solution.py:272
  730.5 50.8 %all_to_all.121 = bf16[3,1024,192]{2,0,1:T(4,128)(2,1)S(1)} all-to-all(bf16[3,1024,192]{2,0,1:T(4,128)(2,1)} %copy.128), channel_id=1, replica_groups=mesh['dp'=8,'seq'=4] {'seq'}, dimensions={1} | all-to-all | bytes 2359296 | tf_op jit(solution)/shard_map/all_to_all | solution.py:279
  793.5 9.0 fusion.93
  802.6 10.6 fusion.102
  817.2 8.6 add_convert_fusion
  849.0 67.9 %reduce-scatter.15.cloned.1.call-done = f32[96,3072]{1,0:T(8,128)} async-done(((f32[768,3072]{1,0:T(8,128)}), f32[96,3072]{1,0:T(8,128)}) %reduce-scatter.15.cloned.1.call-update) | async-done | bytes 1179664 | tf_op jit(solution)/shard_map/reduce_scatter | solution.py:334
  919.0 77.7 %reduce-scatter.17.cloned.1.call-done = f32[384,768]{1,0:T(8,128)} async-done(((f32[3072,768]{1,0:T(8,128)}), f32[384,768]{1,0:T(8,128)}) %reduce-scatter.17.cloned.1.call-update) | async-done | bytes 1179664 | tf_op jit(solution)/shard_map/reduce_scatter | solution.py:336
  1005.2 26.3 %all-reduce.17 = (bf16[768]{0:T(1024)(128)(2,1)}, bf16[768]{0:T(1024)(128)(2,1)}, bf16[768]{0:T(1024)(128)(2,1)}, bf16[768]{0:T(1024)(128)(2,1)}, bf16[768]{0:T(...) all-reduce(f32[768]{0:T(1024)} %get-tuple-element.184, ...), channel_id=2, replica_groups=mesh['dp'=8,'seq'=4] {'dp'}, use_global_device_ids=true, to_apply=%region_16.17.clone | all-reduce | flops 9216 | bytes 55296
  1042.2 13.1 %all-reduce.19 = (bf16[96]{0:T(256)(128)(2,1)}, bf16[96]{0:T(256)(128)(2,1)}, bf16[96]{0:T(256)(128)(2,1)}, bf16[96]{0:T(256)(128)(2,1)}, bf16[96]{0:T(256)(128)...) all-reduce(bf16[96]{0:T(256)(128)(2,1)} %dynamic-slice.43, ...), channel_id=1, replica_groups=mesh['dp'=8,'seq'=4] {'seq'}, use_global_device_ids=true, to_apply=%region_17.18 | all-reduce | flops 1152 | bytes 4608 | tf_op jit(solution)/shard_map/psum | solution.py:356
  1070.8 8.2 all-reduce.23.cloned.1.call-done
  (406 shorter events, 465.6 us)
Async XLA Ops:
  7.2 34.9 %copy-start.1 = (bf16[3,256,768]{2,1,0:T(8,128)(2,1)S(1)}, bf16[3,256,768]{2,1,0:T(8,128)(2,1)}, u32[]{:S(2)}) copy-start(bf16[3,256,768]{2,1,0:T(8,128)(2,1)} %param.22) | copy-start | bytes 3538948
  7.3 35.4 %all-gather.8.cloned.1.call-start = ((), (), s32[]{:S(2)}) async-start(), calls=%async_computation.14 | async-start | bytes 1327104 | tf_op jit(solution)/shard_map/all_gather | solution.py:142
  8.0 54.9 %all-gather.12.cloned.1.call-start = ((), (), s32[]{:S(2)}) async-start(), calls=%async_computation.16 | async-start | bytes 1327104 | tf_op jit(solution)/shard_map/all_gather | solution.py:145
  47.7 38.8 %all-to-all-start = ((bf16[3,256,768]{1,0,2:T(4,128)(2,1)}), bf16[3,256,768]{1,0,2:T(4,128)(2,1)S(1)}, u32[]{:S(2)}, u32[]{:S(2)}) async-start(bf16[3,256,768]{1,0,2:T(4,128)(2,1)} %copy.100), calls=%async_computation | async-start | bytes 3145728 | tf_op jit(solution)/shard_map/all_to_all | solution.py:170
  52.6 38.8 %all-gather.10.cloned.1.call-start = ((), (), s32[]{:S(2)}) async-start(), calls=%async_computation.15 | async-start | bytes 1327104 | tf_op jit(solution)/shard_map/all_gather | solution.py:144
  86.5 40.9 %all-to-all-start.2 = ((bf16[3,256,768]{1,0,2:T(4,128)(2,1)}), bf16[3,256,768]{1,0,2:T(4,128)(2,1)}, u32[]{:S(2)}, u32[]{:S(2)}) async-start(bf16[3,256,768]{1,0,2:T(4,128)(2,1)} %copy.106), calls=%async_computation.2 | async-start | bytes 3145728 | tf_op jit(solution)/shard_map/all_to_all | solution.py:184
  90.8 270.2 %all-gather.14.cloned.1.call-start = ((), (), s32[]{:S(2)}) async-start(), calls=%async_computation.17 | async-start | bytes 1327104 | tf_op jit(solution)/shard_map/all_gather | solution.py:147
  98.7 33.6 %copy-start.26 = (s32[3,256]{1,0:T(4,128)S(1)}, s32[3,256]{1,0:T(4,128)}, u32[]{:S(2)}) copy-start(s32[3,256]{1,0:T(4,128)} %param.23) | copy-start | bytes 9220
  127.3 63.0 %all-to-all-start.1 = ((bf16[3,256,768]{1,0,2:T(4,128)(2,1)}), bf16[3,256,768]{1,0,2:T(4,128)(2,1)}, u32[]{:S(2)}, u32[]{:S(2)}) async-start(bf16[3,256,768]{1,0,2:T(4,128)(2,1)} %copy.103), calls=%async_computation.1 | async-start | bytes 3145728 | tf_op jit(solution)/shard_map/all_to_all | solution.py:177
  131.7 232.6 %all-gather.16.cloned.1.call-start = ((), (), s32[]{:S(2)}) async-start(), calls=%async_computation.18 | async-start | bytes 5308416 | tf_op jit(solution)/shard_map/all_gather | solution.py:151
  305.5 50.2 %all-to-all-start.3 = ((bf16[3,1024,192]{2,0,1:T(4,128)(2,1)}), bf16[3,1024,192]{2,0,1:T(4,128)(2,1)}, u32[]{:S(2)}, u32[]{:S(2)}) async-start(bf16[3,1024,192]{2,0,1:T(4,128)(2,1)} %copy.112), calls=%async_computation.3 | async-start | bytes 4194304 | tf_op jit(solution)/shard_map/all_to_all | solution.py:201
  310.1 81.4 %all-gather.18.cloned.1.call-start = ((), (), s32[]{:S(2)}) async-start(), calls=%async_computation.19 | async-start | bytes 5308416 | tf_op jit(solution)/shard_map/all_gather | solution.py:153
  415.4 40.9 %all-to-all-start.4 = ((bf16[3,256,768]{1,0,2:T(4,128)(2,1)}), bf16[3,256,768]{1,0,2:T(4,128)(2,1)}, u32[]{:S(2)}, u32[]{:S(2)}) async-start(bf16[3,256,768]{1,0,2:T(4,128)(2,1)} %copy.115), calls=%async_computation.4 | async-start | bytes 3145728 | tf_op jit(solution)/shard_map/all_to_all | solution.py:252
  419.8 418.5 %reduce-scatter.13.cloned.1.call-start = ((), (), s32[]{:S(2)}) async-start(), calls=%async_computation.23 | async-start | bytes 2654208 | tf_op jit(solution)/shard_map/reduce_scatter | solution.py:330
  595.3 52.1 %all-to-all-start.5 = ((bf16[3,1024,192]{2,0,1:T(4,128)(2,1)}), bf16[3,1024,192]{2,0,1:T(4,128)(2,1)}, u32[]{:S(2)}, u32[]{:S(2)}) async-start(bf16[3,1024,192]{2,0,1:T(4,128)(2,1)} %copy.122), calls=%async_computation.5 | async-start | bytes 4194304 | tf_op jit(solution)/shard_map/all_to_all | solution.py:265
  599.8 244.3 %reduce-scatter.7.cloned.1.call-start = ((), (), s32[]{:S(2)}) async-start(), calls=%async_computation.20 | async-start | bytes 2654208 | tf_op jit(solution)/shard_map/reduce_scatter | solution.py:325
  659.9 185.7 %reduce-scatter.9.cloned.1.call-start = ((), (), s32[]{:S(2)}) async-start(), calls=%async_computation.21 | async-start | bytes 2654208 | tf_op jit(solution)/shard_map/reduce_scatter | solution.py:327
  726.4 120.9 %reduce-scatter.11.cloned.1.call-start = ((), (), s32[]{:S(2)}) async-start(), calls=%async_computation.22 | async-start | bytes 2654208 | tf_op jit(solution)/shard_map/reduce_scatter | solution.py:328
  793.5 123.4 %reduce-scatter.15.cloned.1.call-start = ((), (), s32[]{:S(2)}) async-start(), calls=%async_computation.24 | async-start | bytes 10616832 | tf_op jit(solution)/shard_map/reduce_scatter | solution.py:334
  802.5 194.2 %reduce-scatter.17.cloned.1.call-start = ((), (), s32[]{:S(2)}) async-start(), calls=%async_computation.25 | async-start | bytes 10616832 | tf_op jit(solution)/shard_map/reduce_scatter | solution.py:336
  813.2 265.8 %all-reduce.23.cloned.1.call-start = ((), (), s32[]{:S(2)}) async-start(), calls=%async_computation.26 | async-start | bytes 3538944 | tf_op jit(solution)/shard_map/psum | solution.py:358
  849.0 149.9 %copy-start.10 = (bf16[768,768]{1,0:T(8,128)(2,1)S(1)}, bf16[768,768]{1,0:T(8,128)(2,1)}, u32[]{:S(2)}) copy-start(bf16[768,768]{1,0:T(8,128)(2,1)} %reshape.310) | copy-start | bytes 3538948
  849.0 149.9 %copy-start.34 = (bf16[768,768]{1,0:T(8,128)(2,1)S(1)}, bf16[768,768]{1,0:T(8,128)(2,1)}, u32[]{:S(2)}) copy-start(bf16[768,768]{1,0:T(8,128)(2,1)} %all-gather.10.cloned.1.call-done) | copy-start | bytes 3538948
  1001.3 65.9 %copy-start.6 = (f32[768,768]{1,0:T(8,128)S(1)}, f32[768,768]{1,0:T(8,128)}, u32[]{:S(2)}) copy-start(f32[768,768]{1,0:T(8,128)} %copy-done.5) | copy-start | bytes 7077892
  (48 other events, 236.2 us)
Sparse Core Ops, SparseCore 0:
  10.0 26.8 all-gather.7
  38.8 24.0 all-gather.11
  64.8 24.0 all-gather.9
  93.2 26.1 all-gather.13
  134.1 41.8 all-gather.15
  312.5 41.8 all-gather.17
  424.5 45.4 reduce-scatter.12
  660.0 43.1 reduce-scatter.6
  726.5 43.1 reduce-scatter.8
  793.6 43.2 reduce-scatter.10
  840.4 76.4 reduce-scatter.14
  920.2 76.4 reduce-scatter.16
  1000.7 78.2 all-reduce.22
where the time goes:
time: 1110 us; the launch traced here: 1090 us
  waiting for transfers between devices  323 us (29%)
  matrix products  266 us (24%)
  blocking collectives  219 us (20%)
  local copies, waits for them, and re-layouts  172 us (15%)
  other arithmetic  68 us (6%)
  starting transfers between devices  27.7 us (2%)
  between operations  16.7 us (2%)
    reduce_scatter x1, waiting for transfers between devices, per_device(): lax.psum_scatter(d_w_down, 'dp', scatter_dimension=0, tiled=True)  77.7 us
    reduce_scatter x1, waiting for transfers between devices, per_device(): lax.psum_scatter(d_w_up, 'dp', scatter_dimension=0, tiled=True)  67.9 us
    unnamed x2, blocking collectives  52.5 us
    all_to_all x1, blocking collectives, per_device(): lax.all_to_all(from_pairs(grad_key_pairs, seqs_here, heads_here), 'seq',...  51.4 us
    all_to_all x1, blocking collectives, per_device(): lax.all_to_all(from_pairs(grad_value_pairs, seqs_here, heads_here), 'seq'...  50.8 us
    all_to_all x1, waiting for transfers between devices, per_device(): lax.all_to_all(from_pairs(grad_query_pairs, seqs_here, heads_here), 'seq'...  45.4 us
    all_gather x1, blocking collectives, per_device(): full_segments = lax.all_gather(segment_ids, 'seq', axis=1, tiled=True)  41.2 us
    dot_general x18, matrix products, masked_scores(): jnp.einsum('qd,kd->qk', query_pair, key_pair, preferred_element_type=jnp....  38.3 us
  transfers between devices with their start and end apart: 19, of which 9 were waited for; matrix products, arithmetic and copies ran while one was open for 41% of the time, Pallas kernels for 0%

commit v1 on v0

--- a/solution.py
+++ b/solution.py
@@ -5,6 +5,29 @@
 
 HD = 64
 EPSILON = 1e-05
+
+
+def split_up(value, dim, size):
+    lengths = value.shape
+    parts = value.reshape(*lengths[:dim], size, lengths[dim] // size, *lengths[dim + 1 :])
+    return jnp.moveaxis(parts, dim, 0)
+
+
+def in_order(blocks, dim):
+    lengths = list(blocks.shape[1:])
+    lengths[dim] *= blocks.shape[0]
+    return jnp.moveaxis(blocks, 0, dim).reshape(lengths)
+
+
+def exchange_in_pairs(value, axis, split_dim, concat_dim):
+    length, index = (lax.axis_size(axis), lax.axis_index(axis))
+    blocks = split_up(value, split_dim, length)
+    outs = [blocks[index]]
+    for step in range(1, length):
+        sent = blocks[index ^ step]
+        outs.append(lax.ppermute(sent, axis, [(i, i ^ step) for i in range(length)]))
+    blocks = jnp.stack(outs)[index ^ jnp.arange(length)]
+    return in_order(blocks, concat_dim)
 
 
 def layer_norm(values, gain, shift):
@@ -167,13 +190,7 @@
         jnp.dot(act_one, w_value, preferred_element_type=jnp.float32) + b_value.astype(jnp.float32)
     ).astype(jnp.bfloat16)
     query_heads, key_heads, value_heads = (
-        lax.all_to_all(
-            query_tok.reshape(seqs_here, positions, model_width),
-            "seq",
-            split_axis=2,
-            concat_axis=1,
-            tiled=True,
-        ),
+        exchange_in_pairs(query_tok.reshape(seqs_here, positions, model_width), "seq", 2, 1),
         lax.all_to_all(
             key_tok.reshape(seqs_here, positions, model_width),
             "seq",

time: 1110 us -> 1100 us (level)
  waiting for transfers between devices: 323 us -> 295 us
  local copies, waits for them, and re-layouts: 172 us -> 191 us
    another operation x4 -> x11, local copies, waits for them, and re-layouts: 4.63 us -> 22.2 us
    all_to_all x1 -> x0, waiting for transfers between devices: 16.2 us -> none  [per_device(): lax.all_to_all(query_tok.reshape(seqs_here, positions, model_width), 'seq...]
    unnamed x115 -> x105, local copies, waits for them, and re-layouts: 17.2 us -> 23.6 us
  transfers between devices with their start and end apart: 19 -> 21, of which waited for: 9 -> 8; matrix products, arithmetic and copies ran while one was open for 41% -> 43% of each run, Pallas kernels for 0% -> 0%
where the time goes in v1:
time: 1100 us; the launch traced here: 1090 us
  waiting for transfers between devices  295 us (27%)
  matrix products  266 us (24%)
  blocking collectives  221 us (20%)
  local copies, waits for them, and re-layouts  191 us (17%)
  other arithmetic  67.8 us (6%)
  starting transfers between devices  27.7 us (3%)
  between operations  16.7 us (2%)
    reduce_scatter x1, waiting for transfers between devices, per_device(): lax.psum_scatter(d_w_down, 'dp', scatter_dimension=0, tiled=True)  77.7 us
    reduce_scatter x1, waiting for transfers between devices, per_device(): lax.psum_scatter(d_w_up, 'dp', scatter_dimension=0, tiled=True)  68.6 us
    unnamed x2, blocking collectives  52.5 us
    all_to_all x1, blocking collectives, per_device(): lax.all_to_all(from_pairs(grad_key_pairs, seqs_here, heads_here), 'seq',...  51.5 us
    all_to_all x1, blocking collectives, per_device(): lax.all_to_all(from_pairs(grad_value_pairs, seqs_here, heads_here), 'seq'...  50.8 us
    all_to_all x1, waiting for transfers between devices, per_device(): lax.all_to_all(from_pairs(grad_query_pairs, seqs_here, heads_here), 'seq'...  45.5 us
    all_gather x1, blocking collectives, per_device(): full_segments = lax.all_gather(segment_ids, 'seq', axis=1, tiled=True)  43.3 us
    dot_general x18, matrix products, masked_scores(): jnp.einsum('qd,kd->qk', query_pair, key_pair, preferred_element_type=jnp....  38.3 us
  transfers between devices with their start and end apart: 21, of which 8 were waited for; matrix products, arithmetic and copies ran while one was open for 43% of the time, Pallas kernels for 0%

profile of v1, /device:TPU:0, one launch (start us, length us, event | category | flops | bytes accessed | tf_op | source)
XLA Modules:
  0.0 1086.0 jit_solution(10602582125430366314)
XLA Ops:
  18.1 26.2 %all-reduce.18 = (bf16[768]{0:T(1024)(128)(2,1)S(1)}, bf16[768]{0:T(1024)(128)(2,1)S(1)}, bf16[768]{0:T(1024)(128)(2,1)S(1)}, bf16[768]{0:T(1024)(128)(2,1)S(1)}...) all-reduce(bf16[768]{0:T(1024)(128)(2,1)S(1)} %dynamic-update-slice, ...), channel_id=1, replica_groups=mesh['dp'=8,'seq'=4] {'dp'}, use_global_device_ids=true, to_apply=%add.1 | all-reduce | flops 6144 | bytes 24576
  52.6 4.9 all-to-all-start.1
  58.0 4.8 all-gather.10.cloned.1.call-done
  70.1 21.2 %all-to-all-done.1 = bf16[3,256,768]{1,0,2:T(4,128)(2,1)S(1)} async-done(((bf16[3,256,768]{1,0,2:T(4,128)(2,1)}), bf16[3,256,768]{1,0,2:T(4,128)(2,1)S(1)}, u32[]{:S(2)}, u32[]{:S(2)}) %all-to-all-start.1) | async-done | bytes 1179680 | tf_op jit(solution)/shard_map/all_to_all | solution.py:201
  119.4 43.3 %all_gather.56 = s32[3,1024]{1,0:T(4,128)S(1)} all-gather(s32[3,256]{1,0:T(4,128)S(1)} %copy-done.30), channel_id=1, replica_groups=mesh['dp'=8,'seq'=4] {'seq'}, dimensions={1}, use_global_device_ids=true | all-gather | bytes 15360 | tf_op jit(solution)/shard_map/all_gather | solution.py:179
  194.4 99.3 %while.26 = (s32[]{:T(128)}, bf16[9,1024,64]{1,2,0:T(8,128)(2,1)}, f32[9,1024]{1,0:T(8,128)}, s32[9,1024]{1,0:T(8,128)}, bf16[9,1024,64]{2,1,0:T(8,128)(2,1)S(1)...) while((s32[]{:T(128)}, bf16[9,1024,64]{1,2,0:T(8,128)(2,1)}, ...), condition=%wide.region_5.6_spmd, body=%wide.region_2.5_spmd.sunk | while | flops 284228608 | bytes 30349440 | solution.py:214
  303.9 10.0 all-gather
  314.5 33.5 %all-to-all-done.2 = bf16[3,1024,192]{2,0,1:T(4,128)(2,1)} async-done(((bf16[3,1024,192]{2,0,1:T(4,128)(2,1)}), bf16[3,1024,192]{2,0,1:T(4,128)(2,1)}, u32[]{:S(2)}, u32[]{:S(2)}) %all-to-all-start.2) | async-done | bytes 1179680 | tf_op jit(solution)/shard_map/all_to_all | solution.py:218
  356.6 27.3 %fusion.56 = (bf16[768,3072]{1,0:T(8,128)(2,1)}, f32[768,3072]{1,0:T(8,128)}) fusion(f32[3072]{0:T(1024)} %bitcast.283, bf16[768,3072]{1,0:T(8,128)(2,1)} %all-gather.16.cloned.1.call-done, f32[768,768]{1,0:T(8,128)S(1)} %get-tuple-element.269, f32[768]{0:T(1024)S(1)} %convert_element_type.227, f32[768]{0:T(1024)S(1)} %convert_element_type.226, ...), kind=kOutput, calls=%fused_computation.65 | convolution fusion | flops 3782541312 | bytes 21258240 | tf_op jit(solution)/shard_map/dot_general | solution.py:230
  383.9 11.6 %convert_reduce_fusion = (f32[3072]{0:T(1024)}, bf16[768,3072]{1,0:T(8,128)(2,1)S(1)}) fusion(f32[768,3072]{1,0:T(8,128)} %get-tuple-element.271, f32[3072]{0:T(1024)} %bitcast.284, bf16[768,768]{1,0:T(8,128)(2,1)} %bitcast.256, bf16[3072,768]{1,0:T(8,128)(2,1)} %all-gather.18.cloned.1.call-done), kind=kOutput, calls=%fused_computation.72 | convolution fusion | flops 3654546432 | bytes 20078592 | tf_op jit(solution)/shard_map/dot_general | solution.py:63
  395.5 4.8 multiply_reduce_fusion.1
  416.8 31.9 %all-to-all-done.3 = bf16[3,256,768]{1,0,2:T(4,128)(2,1)} async-done(((bf16[3,256,768]{1,0,2:T(4,128)(2,1)}), bf16[3,256,768]{1,0,2:T(4,128)(2,1)}, u32[]{:S(2)}, u32[]{:S(2)}) %all-to-all-start.3) | async-done | bytes 1179680 | tf_op jit(solution)/shard_map/all_to_all | solution.py:269
  459.4 124.2 %while.27 = (s32[]{:T(128)}, bf16[9,1024,64]{1,2,0:T(8,128)(2,1)}, bf16[9,1024,64]{1,2,0:T(8,128)(2,1)}, bf16[9,1024,64]{1,2,0:T(8,128)(2,1)}, s32[9,1024]{1,0:T...) while((s32[]{:T(128)}, bf16[9,1024,64]{1,2,0:T(8,128)(2,1)}, ...), condition=%wide.region_12.13_spmd, body=%wide.region_10.12_spmd.sunk | while | flops 681901056 | bytes 33465460 | solution.py:270
  594.4 45.5 %all-to-all-done.4 = bf16[3,1024,192]{2,0,1:T(4,128)(2,1)} async-done(((bf16[3,1024,192]{2,0,1:T(4,128)(2,1)}), bf16[3,1024,192]{2,0,1:T(4,128)(2,1)}, u32[]{:S(2)}, u32[]{:S(2)}) %all-to-all-start.4) | async-done | bytes 1179680 | tf_op jit(solution)/shard_map/all_to_all | solution.py:282
  656.4 51.5 %all_to_all.105 = bf16[3,1024,192]{2,0,1:T(4,128)(2,1)S(1)} all-to-all(bf16[3,1024,192]{2,0,1:T(4,128)(2,1)} %copy.135), channel_id=1, replica_groups=mesh['dp'=8,'seq'=4] {'seq'}, dimensions={1} | all-to-all | bytes 2359296 | tf_op jit(solution)/shard_map/all_to_all | solution.py:289
  722.9 50.8 %all_to_all.106 = bf16[3,1024,192]{2,0,1:T(4,128)(2,1)S(1)} all-to-all(bf16[3,1024,192]{2,0,1:T(4,128)(2,1)} %copy.138), channel_id=1, replica_groups=mesh['dp'=8,'seq'=4] {'seq'}, dimensions={1} | all-to-all | bytes 2359296 | tf_op jit(solution)/shard_map/all_to_all | solution.py:296
  785.9 9.0 fusion.94
  795.0 10.6 fusion.103
  809.3 8.6 add_convert_fusion
  841.1 68.6 %reduce-scatter.15.cloned.1.call-done = f32[96,3072]{1,0:T(8,128)} async-done(((f32[768,3072]{1,0:T(8,128)}), f32[96,3072]{1,0:T(8,128)}) %reduce-scatter.15.cloned.1.call-update) | async-done | bytes 1179664 | tf_op jit(solution)/shard_map/reduce_scatter | solution.py:351
  912.0 77.7 %reduce-scatter.17.cloned.1.call-done = f32[384,768]{1,0:T(8,128)} async-done(((f32[3072,768]{1,0:T(8,128)}), f32[384,768]{1,0:T(8,128)}) %reduce-scatter.17.cloned.1.call-update) | async-done | bytes 1179664 | tf_op jit(solution)/shard_map/reduce_scatter | solution.py:353
  998.1 26.3 %all-reduce.17 = (bf16[768]{0:T(1024)(128)(2,1)}, bf16[768]{0:T(1024)(128)(2,1)}, bf16[768]{0:T(1024)(128)(2,1)}, bf16[768]{0:T(1024)(128)(2,1)}, bf16[768]{0:T(...) all-reduce(f32[768]{0:T(1024)} %get-tuple-element.184, ...), channel_id=2, replica_groups=mesh['dp'=8,'seq'=4] {'dp'}, use_global_device_ids=true, to_apply=%region_16.17.clone | all-reduce | flops 9216 | bytes 55296
  1035.2 13.1 %all-reduce.19 = (bf16[96]{0:T(256)(128)(2,1)}, bf16[96]{0:T(256)(128)(2,1)}, bf16[96]{0:T(256)(128)(2,1)}, bf16[96]{0:T(256)(128)(2,1)}, bf16[96]{0:T(256)(128)...) all-reduce(bf16[96]{0:T(256)(128)(2,1)} %dynamic-slice.63, ...), channel_id=1, replica_groups=mesh['dp'=8,'seq'=4] {'seq'}, use_global_device_ids=true, to_apply=%region_17.18 | all-reduce | flops 1152 | bytes 4608 | tf_op jit(solution)/shard_map/psum | solution.py:373
  1063.7 8.2 all-reduce.23.cloned.1.call-done
  (408 shorter events, 479.4 us)
Async XLA Ops:
  7.2 40.4 %all-gather.12.cloned.1.call-start = ((), (), s32[]{:S(2)}) async-start(), calls=%async_computation.15 | async-start | bytes 1327104 | tf_op jit(solution)/shard_map/all_gather | solution.py:168
  7.9 54.9 %all-gather.10.cloned.1.call-start = ((), (), s32[]{:S(2)}) async-start(), calls=%async_computation.14 | async-start | bytes 1327104 | tf_op jit(solution)/shard_map/all_gather | solution.py:167
  8.7 87.1 %all-gather.8.cloned.1.call-start = ((), (), s32[]{:S(2)}) async-start(), calls=%async_computation.13 | async-start | bytes 1327104 | tf_op jit(solution)/shard_map/all_gather | solution.py:165
  52.6 38.7 %all-to-all-start.1 = ((bf16[3,256,768]{1,0,2:T(4,128)(2,1)}), bf16[3,256,768]{1,0,2:T(4,128)(2,1)S(1)}, u32[]{:S(2)}, u32[]{:S(2)}) async-start(bf16[3,256,768]{1,0,2:T(4,128)(2,1)} %copy.116), calls=%async_computation.1 | async-start | bytes 3145728 | tf_op jit(solution)/shard_map/all_to_all | solution.py:201
  57.4 295.9 %all-gather.14.cloned.1.call-start = ((), (), s32[]{:S(2)}) async-start(), calls=%async_computation.16 | async-start | bytes 1327104 | tf_op jit(solution)/shard_map/all_gather | solution.py:170
  91.3 91.4 %all-to-all-start = ((bf16[3,256,768]{1,0,2:T(4,128)(2,1)}), bf16[3,256,768]{1,0,2:T(4,128)(2,1)}, u32[]{:S(2)}, u32[]{:S(2)}) async-start(bf16[3,256,768]{1,0,2:T(4,128)(2,1)} %copy.113), calls=%async_computation | async-start | bytes 3145728 | tf_op jit(solution)/shard_map/all_to_all | solution.py:194
  95.6 261.0 %all-gather.16.cloned.1.call-start = ((), (), s32[]{:S(2)}) async-start(), calls=%async_computation.17 | async-start | bytes 5308416 | tf_op jit(solution)/shard_map/all_gather | solution.py:174
  110.5 53.4 %collective-permute-start = (bf16[3,256,192]{1,2,0:T(8,128)(2,1)}, bf16[3,256,192]{1,2,0:T(8,128)(2,1)S(1)}, u32[]{:S(2)}, u32[]{:S(2)}) collective-permute-start(bf16[3,256,192]{1,2,0:T(8,128)(2,1)} %bitcast.18), channel_id=1, source_target_pairs={{0,1},{1,0},{2,3},{3,2},{4,5},{5,4},{6,7},{7,6},{8,9},{9,8},{10,11... | collective-permute-start | bytes 884744 | tf_op jit(solution)/shard_map/ppermute | solution.py:28
  115.2 48.7 %collective-permute-start.1 = (bf16[3,256,192]{1,2,0:T(8,128)(2,1)}, bf16[3,256,192]{1,2,0:T(8,128)(2,1)}, u32[]{:S(2)}, u32[]{:S(2)}) collective-permute-start(bf16[3,256,192]{1,2,0:T(8,128)(2,1)} %bitcast.20), channel_id=1, source_target_pairs={{0,2},{1,3},{2,0},{3,1},{4,6},{5,7},{6,4},{7,5},{8,10},{9,11},{10,... | collective-permute-start | bytes 884744 | tf_op jit(solution)/shard_map/ppermute | solution.py:28
  119.2 44.8 %collective-permute-start.2 = (bf16[3,256,192]{1,2,0:T(8,128)(2,1)}, bf16[3,256,192]{1,2,0:T(8,128)(2,1)S(1)}, u32[]{:S(2)}, u32[]{:S(2)}) collective-permute-start(bf16[3,256,192]{1,2,0:T(8,128)(2,1)} %bitcast.22), channel_id=1, source_target_pairs={{0,3},{1,2},{2,1},{3,0},{4,7},{5,6},{6,5},{7,4},{8,11},{9,10},{10,... | collective-permute-start | bytes 884744 | tf_op jit(solution)/shard_map/ppermute | solution.py:28
  298.0 50.0 %all-to-all-start.2 = ((bf16[3,1024,192]{2,0,1:T(4,128)(2,1)}), bf16[3,1024,192]{2,0,1:T(4,128)(2,1)}, u32[]{:S(2)}, u32[]{:S(2)}) async-start(bf16[3,1024,192]{2,0,1:T(4,128)(2,1)} %copy.122), calls=%async_computation.2 | async-start | bytes 4194304 | tf_op jit(solution)/shard_map/all_to_all | solution.py:218
  302.6 81.3 %all-gather.18.cloned.1.call-start = ((), (), s32[]{:S(2)}) async-start(), calls=%async_computation.18 | async-start | bytes 5308416 | tf_op jit(solution)/shard_map/all_gather | solution.py:176
  407.8 40.9 %all-to-all-start.3 = ((bf16[3,256,768]{1,0,2:T(4,128)(2,1)}), bf16[3,256,768]{1,0,2:T(4,128)(2,1)}, u32[]{:S(2)}, u32[]{:S(2)}) async-start(bf16[3,256,768]{1,0,2:T(4,128)(2,1)} %copy.125), calls=%async_computation.3 | async-start | bytes 3145728 | tf_op jit(solution)/shard_map/all_to_all | solution.py:269
  412.1 418.2 %reduce-scatter.13.cloned.1.call-start = ((), (), s32[]{:S(2)}) async-start(), calls=%async_computation.22 | async-start | bytes 2654208 | tf_op jit(solution)/shard_map/reduce_scatter | solution.py:347
  587.7 52.2 %all-to-all-start.4 = ((bf16[3,1024,192]{2,0,1:T(4,128)(2,1)}), bf16[3,1024,192]{2,0,1:T(4,128)(2,1)}, u32[]{:S(2)}, u32[]{:S(2)}) async-start(bf16[3,1024,192]{2,0,1:T(4,128)(2,1)} %copy.132), calls=%async_computation.4 | async-start | bytes 4194304 | tf_op jit(solution)/shard_map/all_to_all | solution.py:282
  592.1 244.0 %reduce-scatter.7.cloned.1.call-start = ((), (), s32[]{:S(2)}) async-start(), calls=%async_computation.19 | async-start | bytes 2654208 | tf_op jit(solution)/shard_map/reduce_scatter | solution.py:342
  652.3 185.5 %reduce-scatter.9.cloned.1.call-start = ((), (), s32[]{:S(2)}) async-start(), calls=%async_computation.20 | async-start | bytes 2654208 | tf_op jit(solution)/shard_map/reduce_scatter | solution.py:344
  718.8 120.7 %reduce-scatter.11.cloned.1.call-start = ((), (), s32[]{:S(2)}) async-start(), calls=%async_computation.21 | async-start | bytes 2654208 | tf_op jit(solution)/shard_map/reduce_scatter | solution.py:345
  785.9 123.9 %reduce-scatter.15.cloned.1.call-start = ((), (), s32[]{:S(2)}) async-start(), calls=%async_computation.23 | async-start | bytes 10616832 | tf_op jit(solution)/shard_map/reduce_scatter | solution.py:351
  795.0 194.7 %reduce-scatter.17.cloned.1.call-start = ((), (), s32[]{:S(2)}) async-start(), calls=%async_computation.24 | async-start | bytes 10616832 | tf_op jit(solution)/shard_map/reduce_scatter | solution.py:353
  805.6 266.3 %all-reduce.23.cloned.1.call-start = ((), (), s32[]{:S(2)}) async-start(), calls=%async_computation.25 | async-start | bytes 3538944 | tf_op jit(solution)/shard_map/psum | solution.py:375
  841.1 150.7 %copy-start.12 = (bf16[768,768]{1,0:T(8,128)(2,1)S(1)}, bf16[768,768]{1,0:T(8,128)(2,1)}, u32[]{:S(2)}) copy-start(bf16[768,768]{1,0:T(8,128)(2,1)} %reshape.324) | copy-start | bytes 3538948
  841.1 150.7 %copy-start.37 = (bf16[768,768]{1,0:T(8,128)(2,1)S(1)}, bf16[768,768]{1,0:T(8,128)(2,1)}, u32[]{:S(2)}) copy-start(bf16[768,768]{1,0:T(8,128)(2,1)} %all-gather.10.cloned.1.call-done) | copy-start | bytes 3538948
  994.3 65.9 %copy-start.6 = (f32[768,768]{1,0:T(8,128)S(1)}, f32[768,768]{1,0:T(8,128)}, u32[]{:S(2)}) copy-start(f32[768,768]{1,0:T(8,128)} %copy-done.5) | copy-start | bytes 7077892
  (45 other events, 186.9 us)
Sparse Core Ops, SparseCore 0:
  9.9 26.8 all-gather.11
  38.7 24.0 all-gather.9
  64.7 24.0 all-gather.7
  90.5 24.0 all-gather.13
  119.5 40.9 all-gather.15
  305.0 41.7 all-gather.17
  416.9 46.0 reduce-scatter.12
  652.4 43.7 reduce-scatter.6
  718.9 43.6 reduce-scatter.8
  786.0 43.7 reduce-scatter.10
  833.3 76.4 reduce-scatter.14
  913.1 76.4 reduce-scatter.16
  993.7 78.2 all-reduce.22
